TPU v7x, 128 devices: a whole 4x4x4 slice. The times are simulated.
128 devices in a mesh: ctx: 8 (over x, z_lo), head: 16 (over z_hi, y, core).
Axes of the slice: x: 4, y: 4, z: 4 (z_hi: 2, z_lo: 2; z = z_hi * 2 + z_lo), core: 2. Of those that a mesh axis runs over, the one named last changes fastest.
Arguments:
- queries: bfloat16 [256, 16384], P(None, 'head'), may hold values from -64 to 64, as said below
- grad_out: bfloat16 [256, 16384], P(None, 'head'), may hold values from -24 to 24
- latent: bfloat16 [16384, 512], P(('ctx', 'head')), may hold values from -6.1 to 6.1
- up_key: bfloat16 [512, 16384], P(None, 'head'), as said below
- up_value: bfloat16 [512, 16384], P(None, 'head'), may hold values from -0.25 to 0.25
Outputs:
- grad_queries: float32 [256, 16384], P('ctx', 'head')
- grad_latent: float32 [16384, 512], P(('ctx', 'head'))
- grad_up_key: float32 [512, 16384], P('ctx', 'head')
- grad_up_value: float32 [512, 16384], P('ctx', 'head')
Inputs may be any that keep to these rules, and one draw needn't show every extreme that they name: `queries`: entries lie within 64 in magnitude. `up_key`: entries lie within 4 / sqrt(512) in magnitude.
All inputs are finite; a program needn't handle non-finite values.
Results may differ from a plain program's by a relative error of at most 0.005.
Values may be sent and summed in bfloat16 or wider, within the bound.
A program may use at most 128 MiB of HBM per device.

v0:
```python
import math
import jax
import jax.numpy as jnp
from jax import lax
from jax.sharding import PartitionSpec as P

HD = 128


def joined(part, axis, combine):
    gathered = jax.tree.map(lambda a: lax.all_gather(a, axis), part)

    def take(source):
        return jax.tree.map(lambda a: lax.dynamic_index_in_dim(a, source, 0, False), gathered)

    return lax.fori_loop(
        1, lax.axis_size(axis), lambda source, state: combine(state, take(source)), take(0)
    )


def join_pairs(former, latter):
    maxima = jnp.maximum(former[0], latter[0])
    left_factor = jnp.exp(former[0] - maxima)
    right_factor = jnp.exp(latter[0] - maxima)
    return (maxima, former[1] * left_factor + latter[1] * right_factor)


def local(queries, grad_out, latent, up_key, up_value):
    scale = 1.0 / math.sqrt(HD)
    local_heads = queries.shape[1] // HD
    width = queries.shape[1]
    query_count = queries.shape[0]
    contract_cols = (((1,), (1,)), ((), ()))
    contract_rows = (((0,), (0,)), ((), ()))
    block = lax.all_gather(latent, "head", axis=0, tiled=True)
    key_rows = block.shape[0]
    total_len = key_rows * lax.axis_size("ctx")
    first_key = lax.axis_index("ctx") * key_rows
    key_block = jnp.dot(block, up_key, preferred_element_type=jnp.float32)
    value_block = jnp.dot(block, up_value, preferred_element_type=jnp.float32).astype(jnp.bfloat16)
    query_pos = total_len - query_count + lax.iota(jnp.int32, query_count)
    key_pos = first_key + lax.iota(jnp.int32, key_rows)
    visible = key_pos[None, :] <= query_pos[:, None]
    head_ids = jnp.arange(local_heads, dtype=jnp.int32)

    def head_inputs(head_index):
        offset = head_index * HD
        return (
            lax.dynamic_slice_in_dim(queries, offset, HD, 1),
            lax.dynamic_slice_in_dim(grad_out, offset, HD, 1),
            lax.dynamic_slice_in_dim(key_block, offset, HD, 1),
            lax.dynamic_slice_in_dim(value_block, offset, HD, 1),
        )

    def masked_scores(query_head, key_head):
        raw = (
            lax.dot_general(
                query_head.astype(jnp.float32),
                key_head,
                contract_cols,
                precision=lax.Precision.HIGHEST,
            )
            * scale
        )
        return jnp.where(visible, raw, -jnp.inf)

    def product_scores(grad_head, value_head):
        return lax.dot_general(
            grad_head, value_head, contract_cols, preferred_element_type=jnp.float32
        )

    def pick_row(table, head_index):
        return lax.dynamic_index_in_dim(table, head_index, 0, keepdims=False)

    def local_pair(head_index):
        query_head, grad_head, key_head, value_head = head_inputs(head_index)
        scores = masked_scores(query_head, key_head)
        maxima = jnp.max(scores, axis=1)
        return (maxima, jnp.sum(jnp.exp(scores - maxima[:, None]), axis=1))

    local_max, local_sum = lax.map(local_pair, head_ids)
    maxima, totals = joined((local_max, local_sum), "ctx", join_pairs)

    def local_delta(head_index):
        query_head, grad_head, key_head, value_head = head_inputs(head_index)
        scores = masked_scores(query_head, key_head)
        probs = (
            jnp.exp(scores - pick_row(maxima, head_index)[:, None])
            / pick_row(totals, head_index)[:, None]
        )
        return jnp.sum(probs * product_scores(grad_head, value_head), axis=1)

    deltas = lax.psum(lax.map(local_delta, head_ids), "ctx")

    def accumulate(head_index, carry):
        query_acc, grad_kv = carry
        query_head, grad_head, key_head, value_head = head_inputs(head_index)
        scores = masked_scores(query_head, key_head)
        probs = (
            jnp.exp(scores - pick_row(maxima, head_index)[:, None])
            / pick_row(totals, head_index)[:, None]
        )
        grad_probs = product_scores(grad_head, value_head)
        grad_scores = (probs * (grad_probs - pick_row(deltas, head_index)[:, None]) * scale).astype(
            jnp.bfloat16
        )
        query_part = jnp.dot(
            grad_scores.astype(jnp.float32), key_head, precision=lax.Precision.HIGHEST
        )
        key_grad = lax.dot_general(
            grad_scores, query_head, contract_rows, preferred_element_type=jnp.float32
        ).astype(jnp.bfloat16)
        value_grad = lax.dot_general(
            probs.astype(jnp.bfloat16), grad_head, contract_rows, preferred_element_type=jnp.float32
        ).astype(jnp.bfloat16)
        offset = head_index * HD
        anchor = jnp.zeros((), jnp.int32)
        query_acc = lax.dynamic_update_slice(query_acc, query_part, (anchor, offset))
        grad_kv = lax.dynamic_update_slice(grad_kv, key_grad, (anchor, offset))
        grad_kv = lax.dynamic_update_slice(grad_kv, value_grad, (anchor, width + offset))
        return (query_acc, grad_kv)

    start_state = (
        jnp.zeros((query_count, width), jnp.float32),
        jnp.zeros((key_rows, 2 * width), jnp.bfloat16),
    )
    query_acc, grad_kv = lax.fori_loop(0, local_heads, accumulate, start_state)
    up_both = jnp.concatenate([up_key, up_value], axis=1)
    grad_queries = lax.psum_scatter(query_acc, "ctx", scatter_dimension=0, tiled=True)
    weight_sums = lax.psum_scatter(
        lax.dot_general(block, grad_kv, contract_rows, preferred_element_type=jnp.float32),
        "ctx",
        scatter_dimension=0,
        tiled=True,
    )
    own_rows = latent.shape[0]
    summed = lax.psum(
        lax.dot_general(grad_kv, up_both, contract_cols, preferred_element_type=jnp.float32), "head"
    )
    grad_latent = lax.dynamic_slice_in_dim(summed, lax.axis_index("head") * own_rows, own_rows, 0)
    return (grad_queries, grad_latent, weight_sums[:, :width], weight_sums[:, width:])


def solution(mesh):
    return jax.shard_map(
        local,
        mesh=mesh,
        in_specs=(
            P(None, "head"),
            P(None, "head"),
            P(("ctx", "head"), None),
            P(None, "head"),
            P(None, "head"),
        ),
        out_specs=(P("ctx", "head"), P(("ctx", "head"), None), P("ctx", "head"), P("ctx", "head")),
        check_vma=False,
    )
```

profile of v0, /device:TPU:0, one launch (start us, length us, event | category | flops | bytes accessed | tf_op | source)
XLA Modules:
  0.0 633.1 jit_solution(3696228629027708976)
XLA Ops:
  8.0 53.2 %all-gather.4.cloned.1.call-done = bf16[2048,512]{1,0:T(8,128)(2,1)} async-done(((bf16[128,512]{1,0:T(8,128)(2,1)}), bf16[2048,512]{1,0:T(8,128)(2,1)}) %all-gather.4.cloned.1.call-update) | async-done | bytes 2097168 | tf_op jit(solution)/shard_map/all_gather | solution.py:35
  61.2 7.4 %fusion.52 = f32[2048,1024]{1,0:T(8,128)} fusion(bf16[2048,512]{1,0:T(8,128)(2,1)} %all-gather.4.cloned.1.call-done, bf16[512,1024]{1,0:T(8,128)(2,1)} %param.16), kind=kOutput, calls=%fused_computation.71 | convolution fusion | flops 2147483648 | bytes 11534336 | tf_op jit(solution)/shard_map/dot_general | solution.py:39
  68.6 34.9 %while.60 = (s32[]{:T(128)}, f32[8,256]{1,0:T(8,128)S(1)}, f32[8,256]{1,0:T(8,128)S(1)}, s32[8]{0:T(128)S(1)}, bf16[256,1024]{1,0:T(8,128)(2,1)S(1)}, /*index=5*...) while((s32[]{:T(128)}, f32[8,256]{1,0:T(8,128)S(1)}, ...), condition=%wide.region_3.4_spmd.clone, body=%wide.region_0.3_spmd.clone.sunk | while | flops 808451584 | bytes 5326015 | solution.py:81
  103.6 28.2 %all-gather.1 = f32[64,256]{1,0:T(8,128)S(1)} all-gather(f32[8,256]{1,0:T(8,128)S(1)} %get-tuple-element.493), channel_id=3, replica_groups=mesh['ctx'=8,'head'=16] {'ctx'}, dimensions={0}, use_global_device_ids=true | all-gather | bytes 73728 | tf_op jit(solution)/shard_map/all_gather | solution.py:11
  131.8 28.2 %all-gather = f32[64,256]{1,0:T(8,128)S(1)} all-gather(f32[8,256]{1,0:T(8,128)S(1)} %get-tuple-element.492), channel_id=2, replica_groups=mesh['ctx'=8,'head'=16] {'ctx'}, dimensions={0}, use_global_device_ids=true | all-gather | bytes 73728 | tf_op jit(solution)/shard_map/all_gather | solution.py:11
  160.2 5.9 convolution_convert_fusion.2
  166.1 60.3 %while.61 = (s32[]{:T(128)}, f32[8,256]{1,0:T(8,128)S(1)}, s32[8]{0:T(128)S(1)}, bf16[256,1024]{1,0:T(8,128)(2,1)S(1)}, f32[2048,1024]{1,0:T(8,128)}, /*index=5*...) while((s32[]{:T(128)}, f32[8,256]{1,0:T(8,128)S(1)}, ...), condition=%wide.region_8.9_spmd.clone, body=%wide.region_6.8_spmd.clone.sunk | while | flops 943193856 | bytes 5918977 | solution.py:93
  226.5 19.1 %psum.14 = f32[8,256]{1,0:T(8,128)S(1)} all-reduce(f32[8,256]{1,0:T(8,128)S(1)} %get-tuple-element.496), channel_id=1, replica_groups=mesh['ctx'=8,'head'=16] {'ctx'}, use_global_device_ids=true, to_apply=%region_9.10 | all-reduce | flops 2048 | bytes 16384 | tf_op jit(solution)/shard_map/psum | solution.py:93
  245.7 4.3 broadcast_in_dim.48
  250.0 80.9 %while.62 = (s32[]{:T(128)}, f32[256,1024]{1,0:T(8,128)S(1)}, bf16[2048,2048]{1,0:T(8,128)(2,1)}, bf16[256,1024]{1,0:T(8,128)(2,1)S(1)}, f32[2048,1024]{1,0:T(8,...) while((s32[]{:T(128)}, f32[256,1024]{1,0:T(8,128)S(1)}, ...), condition=%wide.region_11.12_spmd.clone, body=%wide.region_10.11_spmd.clone.sunk | while | flops 2019033088 | bytes 13522222 | solution.py:127
  250.0 2.8 fusion.102
  260.2 2.7 fusion.102
  270.3 2.7 fusion.102
  280.4 2.7 fusion.102
  290.5 2.7 fusion.102
  300.6 2.7 fusion.102
  310.7 2.7 fusion.102
  320.8 2.7 fusion.102
  330.9 10.5 %fusion.45 = f32[2048,512]{1,0:T(8,128)} fusion(bf16[2048,2048]{1,0:T(8,128)(2,1)} %get-tuple-element.498, bf16[512,1024]{1,0:T(8,128)(2,1)} %param.17, bf16[512,1024]{1,0:T(8,128)(2,1)S(1)} %copy-done.3), kind=kOutput, calls=%fused_computation.61 | convolution fusion | flops 4299161600 | bytes 14680064 | tf_op jit(solution)/shard_map/dot_general | solution.py:138
  343.0 9.8 %convolution_bitcast_fusion = f32[512,2048]{0,1:T(8,128)} fusion(bf16[2048,2048]{1,0:T(8,128)(2,1)} %get-tuple-element.498, bf16[2048,512]{1,0:T(8,128)(2,1)S(1)} %copy-done.2), kind=kOutput, calls=%fused_computation.60 | convolution fusion | flops 4294967296 | bytes 14680064 | tf_op jit(solution)/shard_map/dot_general | solution.py:131
  352.8 5.5 copy.13
  358.8 130.5 %all-reduce.2.cloned.1.call-done = f32[2048,512]{1,0:T(8,128)} async-done(((f32[2048,512]{1,0:T(8,128)}), f32[2048,512]{1,0:T(8,128)}) %all-reduce.2.cloned.1.call-update) | async-done | bytes 4194320 | tf_op jit(solution)/shard_map/psum | solution.py:137
  491.1 91.7 %reduce-scatter.7.cloned.1.call-done = f32[64,2048]{1,0:T(8,128)} async-done(((f32[512,2048]{1,0:T(8,128)}), f32[64,2048]{1,0:T(8,128)}) %reduce-scatter.7.cloned.1.call-update) | async-done | bytes 524304
  584.6 41.9 %reduce-scatter.5.cloned.1.call-done = f32[32,1024]{1,0:T(8,128)} async-done(((f32[256,1024]{1,0:T(8,128)}), f32[32,1024]{1,0:T(8,128)}) %reduce-scatter.5.cloned.1.call-update) | async-done | bytes 131088 | tf_op jit(solution)/shard_map/reduce_scatter | solution.py:129
  (166 shorter events, 135.0 us)
Async XLA Ops:
  7.2 54.0 %all-gather.4.cloned.1.call-start = ((), (), s32[]{:S(2)}) async-start(), calls=%async_computation.2 | async-start | bytes 2228224 | tf_op jit(solution)/shard_map/all_gather | solution.py:35
  7.9 481.5 %all-reduce.2.cloned.1.call-start = ((), (), s32[]{:S(2)}) async-start(), calls=%async_computation.4 | async-start | bytes 8388608 | tf_op jit(solution)/shard_map/psum | solution.py:137
  8.0 60.7 %copy-start.1 = (bf16[256,1024]{1,0:T(8,128)(2,1)S(1)}, bf16[256,1024]{1,0:T(8,128)(2,1)}, u32[]{:S(2)}) copy-start(bf16[256,1024]{1,0:T(8,128)(2,1)} %param.13) | copy-start | bytes 1572868
  68.6 91.6 %copy-start.4 = (bf16[512,1024]{1,0:T(8,128)(2,1)S(1)}, bf16[512,1024]{1,0:T(8,128)(2,1)}, u32[]{:S(2)}) copy-start(bf16[512,1024]{1,0:T(8,128)(2,1)} %param.17) | copy-start | bytes 3145732
  250.0 80.9 %copy-start.3 = (bf16[512,1024]{1,0:T(8,128)(2,1)S(1)}, bf16[512,1024]{1,0:T(8,128)(2,1)}, u32[]{:S(2)}) copy-start(bf16[512,1024]{1,0:T(8,128)(2,1)} %param.16) | copy-start | bytes 3145732
  330.9 10.5 %copy-start = (f32[256,1024]{1,0:T(8,128)}, f32[256,1024]{1,0:T(8,128)S(1)}, u32[]{:S(2)}) copy-start(f32[256,1024]{1,0:T(8,128)S(1)} %get-tuple-element.497) | copy-start | bytes 3145732
  341.4 1.6 copy-start.2
  341.4 241.3 %reduce-scatter.7.cloned.1.call-start = ((), (), s32[]{:S(2)}) async-start(), calls=%async_computation.5 | async-start | bytes 4718592
  358.3 268.3 %reduce-scatter.5.cloned.1.call-start = ((), (), s32[]{:S(2)}) async-start(), calls=%async_computation.3 | async-start | bytes 1179648 | tf_op jit(solution)/shard_map/reduce_scatter | solution.py:129
Sparse Core Ops, SparseCore 0:
  10.4 50.7 all-gather.3
  341.6 147.7 all-reduce.1
  491.8 90.8 reduce-scatter.6
  585.5 40.9 reduce-scatter.4
where the time goes:
time: 636 us; the launch traced here: 633 us
  waiting for transfers between devices  319 us (50%)
  matrix products  169 us (27%)
  blocking collectives  75.5 us (12%)
  loops' own time  26.6 us (4%)
  local copies, waits for them, and re-layouts  25.9 us (4%)
  between operations  13.9 us (2%)
    psum x1, waiting for transfers between devices, local(): lax.psum(lax.dot_general(grad_kv, up_both, contract_cols, preferred_eleme...  131 us
    unnamed x5, waiting for transfers between devices  92.9 us
    dot_general x24, matrix products, masked_scores(): lax.dot_general(query_head.astype(jnp.float32), key_head, contract_cols,...  63.4 us
    all_gather x2, blocking collectives, joined(): gathered = jax.tree.map(lambda a: lax.all_gather(a, axis), part)  56.4 us
    all_gather x1, waiting for transfers between devices, local(): block = lax.all_gather(latent, 'head', axis=0, tiled=True)  53.2 us
    reduce_scatter x1, waiting for transfers between devices, local(): lax.psum_scatter(query_acc, 'ctx', scatter_dimension=0, tiled=True)  41.9 us
    dot_general x16, matrix products, product_scores(): lax.dot_general(grad_head, value_head, contract_cols, preferred_element_t...  25.1 us
    another operation x1, loops' own time, local(): deltas = lax.psum(lax.map(local_delta, head_ids), 'ctx')  21 us
  transfers between devices with their start and end apart: 4, of which 4 were waited for; matrix products, arithmetic and copies ran while one was open for 3% of the time, Pallas kernels for 0%

commit v1 on v0

--- a/solution.py
+++ b/solution.py
@@ -134,9 +134,9 @@
         tiled=True,
     )
     own_rows = latent.shape[0]
-    summed = lax.psum(
-        lax.dot_general(grad_kv, up_both, contract_cols, preferred_element_type=jnp.float32), "head"
-    )
+    part_2 = lax.dot_general(grad_kv, up_both, contract_cols, preferred_element_type=jnp.float32)
+    parts = lax.all_gather(part_2, "head", axis=0, tiled=False)
+    summed = parts.sum(axis=0)
     grad_latent = lax.dynamic_slice_in_dim(summed, lax.axis_index("head") * own_rows, own_rows, 0)
     return (grad_queries, grad_latent, weight_sums[:, :width], weight_sums[:, width:])
 

time: 636 us -> 830 us (1.31)
  waiting for transfers between devices: 319 us -> 489 us
  other arithmetic: 3.64 us -> 26.9 us
    all_gather x0 -> x1, waiting for transfers between devices: none -> 344 us  [local(): parts = lax.all_gather(part_2, 'head', axis=0, tiled=False)]
    psum x1 -> x0, waiting for transfers between devices: 131 us -> none  [local(): lax.psum(lax.dot_general(grad_kv, up_both, contract_cols, preferred_eleme...]
    reduce_scatter x1, waiting for transfers between devices: 41.9 us -> 14.8 us  [local(): lax.psum_scatter(query_acc, 'ctx', scatter_dimension=0, tiled=True)]
    reduce_sum x0 -> x1, other arithmetic: none -> 23.3 us  [local(): summed = parts.sum(axis=0)]
    unnamed x5, waiting for transfers between devices: 92.9 us -> 77.4 us
  transfers between devices with their start and end apart: 4 -> 4, of which waited for: 4 -> 4; matrix products, arithmetic and copies ran while one was open for 3% -> 4% of each run, Pallas kernels for 0% -> 0%
where the time goes in v1:
time: 830 us; the launch traced here: 827 us
  waiting for transfers between devices  489 us (59%)
  matrix products  169 us (20%)
  blocking collectives  75.5 us (9%)
  loops' own time  27.1 us (3%)
  other arithmetic  26.9 us (3%)
  local copies, waits for them, and re-layouts  25.6 us (3%)
  between operations  13.9 us (2%)
    all_gather x1, waiting for transfers between devices, local(): parts = lax.all_gather(part_2, 'head', axis=0, tiled=False)  344 us
    unnamed x5, waiting for transfers between devices  77.4 us
    dot_general x24, matrix products, masked_scores(): lax.dot_general(query_head.astype(jnp.float32), key_head, contract_cols,...  63.3 us
    all_gather x2, blocking collectives, joined(): gathered = jax.tree.map(lambda a: lax.all_gather(a, axis), part)  56.4 us
    all_gather x1, waiting for transfers between devices, local(): block = lax.all_gather(latent, 'head', axis=0, tiled=True)  53.2 us
    dot_general x16, matrix products, product_scores(): lax.dot_general(grad_head, value_head, contract_cols, preferred_element_t...  25.1 us
    reduce_sum x1, other arithmetic, local(): summed = parts.sum(axis=0)  23.3 us
    another operation x1, loops' own time, local(): deltas = lax.psum(lax.map(local_delta, head_ids), 'ctx')  21 us
  transfers between devices with their start and end apart: 4, of which 4 were waited for; matrix products, arithmetic and copies ran while one was open for 4% of the time, Pallas kernels for 0%

profile of v1, /device:TPU:0, one launch (start us, length us, event | category | flops | bytes accessed | tf_op | source)
XLA Modules:
  0.0 827.1 jit_solution(1151273844812888880)
XLA Ops:
  8.0 53.2 %all-gather.6.cloned.1.call-done = bf16[2048,512]{1,0:T(8,128)(2,1)} async-done(((bf16[128,512]{1,0:T(8,128)(2,1)}), bf16[2048,512]{1,0:T(8,128)(2,1)}) %all-gather.6.cloned.1.call-update) | async-done | bytes 2097168 | tf_op jit(solution)/shard_map/all_gather | solution.py:35
  61.2 7.4 fusion.52
  68.6 35.4 %while.60 = (s32[]{:T(128)}, f32[8,256]{1,0:T(8,128)S(1)}, f32[8,256]{1,0:T(8,128)S(1)}, s32[8]{0:T(128)S(1)}, bf16[256,1024]{1,0:T(8,128)(2,1)S(1)}, /*index=5*...) while((s32[]{:T(128)}, f32[8,256]{1,0:T(8,128)S(1)}, ...), condition=%wide.region_3.4_spmd.clone, body=%wide.region_0.3_spmd.clone.sunk | while | flops 808451584 | bytes 5326015 | solution.py:81
  104.1 28.2 %all-gather.1 = f32[64,256]{1,0:T(8,128)S(1)} all-gather(f32[8,256]{1,0:T(8,128)S(1)} %get-tuple-element.493), channel_id=3, replica_groups=mesh['ctx'=8,'head'=16] {'ctx'}, dimensions={0}, use_global_device_ids=true | all-gather | bytes 73728 | tf_op jit(solution)/shard_map/all_gather | solution.py:11
  132.3 28.2 %all-gather = f32[64,256]{1,0:T(8,128)S(1)} all-gather(f32[8,256]{1,0:T(8,128)S(1)} %get-tuple-element.492), channel_id=2, replica_groups=mesh['ctx'=8,'head'=16] {'ctx'}, dimensions={0}, use_global_device_ids=true | all-gather | bytes 73728 | tf_op jit(solution)/shard_map/all_gather | solution.py:11
  160.8 5.9 convolution_convert_fusion.2
  166.7 60.3 %while.61 = (s32[]{:T(128)}, f32[8,256]{1,0:T(8,128)S(1)}, s32[8]{0:T(128)S(1)}, bf16[256,1024]{1,0:T(8,128)(2,1)S(1)}, f32[2048,1024]{1,0:T(8,128)}, /*index=5*...) while((s32[]{:T(128)}, f32[8,256]{1,0:T(8,128)S(1)}, ...), condition=%wide.region_8.9_spmd.clone, body=%wide.region_6.8_spmd.clone.sunk | while | flops 943193856 | bytes 5918977 | solution.py:93
  227.0 19.1 %psum.7 = f32[8,256]{1,0:T(8,128)S(1)} all-reduce(f32[8,256]{1,0:T(8,128)S(1)} %get-tuple-element.496), channel_id=1, replica_groups=mesh['ctx'=8,'head'=16] {'ctx'}, use_global_device_ids=true, to_apply=%region_9.10 | all-reduce | flops 2048 | bytes 16384 | tf_op jit(solution)/shard_map/psum | solution.py:93
  246.2 4.3 broadcast_in_dim.48
  250.5 80.8 %while.62 = (s32[]{:T(128)}, f32[256,1024]{1,0:T(8,128)S(1)}, bf16[2048,2048]{1,0:T(8,128)(2,1)}, bf16[256,1024]{1,0:T(8,128)(2,1)S(1)}, f32[2048,1024]{1,0:T(8,...) while((s32[]{:T(128)}, f32[256,1024]{1,0:T(8,128)S(1)}, ...), condition=%wide.region_11.12_spmd.clone, body=%wide.region_10.11_spmd.clone.sunk | while | flops 2019033088 | bytes 13522222 | solution.py:127
  250.5 2.7 fusion.102
  260.6 2.7 fusion.102
  270.7 2.7 fusion.102
  280.8 2.7 fusion.102
  301.0 2.7 fusion.102
  311.1 2.7 fusion.102
  321.2 2.7 fusion.102
  331.3 10.8 %convolution_bitcast_fusion = f32[512,2048]{0,1:T(8,128)} fusion(bf16[2048,2048]{1,0:T(8,128)(2,1)} %get-tuple-element.498, bf16[2048,512]{1,0:T(8,128)(2,1)} %all-gather.6.cloned.1.call-done), kind=kOutput, calls=%fused_computation.60 | convolution fusion | flops 4294967296 | bytes 14680064 | tf_op jit(solution)/shard_map/dot_general | solution.py:131
  342.1 5.5 copy.13
  348.8 9.6 %fusion.45 = f32[2048,512]{1,0:T(8,128)} fusion(bf16[2048,2048]{1,0:T(8,128)(2,1)} %get-tuple-element.498, bf16[512,1024]{1,0:T(8,128)(2,1)S(1)} %copy-done.3, bf16[512,1024]{1,0:T(8,128)(2,1)S(1)} %copy-done.2), kind=kOutput, calls=%fused_computation.61 | convolution fusion | flops 4299161600 | bytes 14680064 | tf_op jit(solution)/shard_map/dot_general | solution.py:137
  359.1 76.2 %reduce-scatter.7.cloned.1.call-done = f32[64,2048]{1,0:T(8,128)} async-done(((f32[512,2048]{1,0:T(8,128)}), f32[64,2048]{1,0:T(8,128)}) %reduce-scatter.7.cloned.1.call-update) | async-done | bytes 524304
  437.1 343.7 %all-gather.8.cloned.1.call-done = f32[32768,512]{1,0:T(8,128)} async-done(((f32[2048,512]{1,0:T(8,128)}), f32[32768,512]{1,0:T(8,128)}) %all-gather.8.cloned.1.call-update) | async-done | bytes 67108880 | tf_op jit(solution)/shard_map/all_gather | solution.py:138
  780.8 23.3 %reduce_sum.27 = f32[2048,512]{1,0:T(8,128)} reduce(f32[16,2048,512]{2,1,0:T(8,128)} %bitcast.4, f32[]{:T(128)} %constant.194.clone.1), dimensions={0}, to_apply=%region_13.14 | reduce | flops 15728640 | bytes 71303168 | tf_op jit(solution)/shard_map/reduce_sum | solution.py:139
  805.8 14.8 %reduce-scatter.5.cloned.1.call-done = f32[32,1024]{1,0:T(8,128)} async-done(((f32[256,1024]{1,0:T(8,128)}), f32[32,1024]{1,0:T(8,128)}) %reduce-scatter.5.cloned.1.call-update) | async-done | bytes 131088 | tf_op jit(solution)/shard_map/reduce_scatter | solution.py:129
  (165 shorter events, 137.4 us)
Async XLA Ops:
  7.2 54.0 %all-gather.6.cloned.1.call-start = ((), (), s32[]{:S(2)}) async-start(), calls=%async_computation.2 | async-start | bytes 2228224 | tf_op jit(solution)/shard_map/all_gather | solution.py:35
  7.9 427.3 %reduce-scatter.7.cloned.1.call-start = ((), (), s32[]{:S(2)}) async-start(), calls=%async_computation.5 | async-start | bytes 4718592
  8.0 60.6 %copy-start.1 = (bf16[256,1024]{1,0:T(8,128)(2,1)S(1)}, bf16[256,1024]{1,0:T(8,128)(2,1)}, u32[]{:S(2)}) copy-start(bf16[256,1024]{1,0:T(8,128)(2,1)} %param.13) | copy-start | bytes 1572868
  68.6 92.1 %copy-start.3 = (bf16[512,1024]{1,0:T(8,128)(2,1)S(1)}, bf16[512,1024]{1,0:T(8,128)(2,1)}, u32[]{:S(2)}) copy-start(bf16[512,1024]{1,0:T(8,128)(2,1)} %param.17) | copy-start | bytes 3145732
  331.3 10.9 %copy-start = (f32[256,1024]{1,0:T(8,128)}, f32[256,1024]{1,0:T(8,128)S(1)}, u32[]{:S(2)}) copy-start(f32[256,1024]{1,0:T(8,128)S(1)} %get-tuple-element.497) | copy-start | bytes 3145732
  347.6 1.2 copy-start.2
  347.6 433.2 %all-gather.8.cloned.1.call-start = ((), (), s32[]{:S(2)}) async-start(), calls=%async_computation.4 | async-start | bytes 71303168 | tf_op jit(solution)/shard_map/all_gather | solution.py:138
  358.5 462.1 %reduce-scatter.5.cloned.1.call-start = ((), (), s32[]{:S(2)}) async-start(), calls=%async_computation.3 | async-start | bytes 1179648 | tf_op jit(solution)/shard_map/reduce_scatter | solution.py:129
Sparse Core Ops, SparseCore 0:
  10.4 50.7 all-gather.5
  347.8 87.4 reduce-scatter.6
  437.7 343.0 all-gather.7
  783.6 36.9 reduce-scatter.4
